TPU v7x, 32 devices: a whole 2x2x4 slice. The times are simulated.
32 devices in a mesh: group: 2 (over x), expert: 16 (over z, y, core).
Axes of the slice: x: 2, y: 2, z: 4, core: 2. Of those that a mesh axis runs over, the one named last changes fastest.
Arguments:
- tokens: bfloat16 [64, 256, 1024], P(('group', 'expert')), parts along dimension 0, may hold values from -6 to 6
- w_qkv: bfloat16 [1024, 3072], P('expert'), may hold values from -0.1875 to 0.1875
- w_attn_out: bfloat16 [1024, 1024], P('expert'), may hold values from -0.1875 to 0.1875
- slot_keys: bfloat16 [1024, 32], replicated, may hold values from -0.5 to 0.5
- w_expert_in: bfloat16 [16, 1024, 2048], P('expert'), may hold values from -0.375 to 0.375
- w_expert_out: bfloat16 [16, 2048, 1024], P('expert'), may hold values from -0.125 to 0.125
Outputs:
- block_out: bfloat16 [64, 256, 1024], P(('group', 'expert')), parts along dimension 0
There are 2 independent parts, one for each index of `group`. A program takes and returns all parts, laid end to end along the dimension named above; an argument that names none is the same for every part. Nothing has to cross between parts.
All inputs are finite; a program needn't handle non-finite values.
Results may differ from a plain program's by a relative error of at most 0.009.
Values may be sent and summed in bfloat16 or wider, within the bound.
No kernel may reach another device: no remote copies, remote signals or barrier semaphores. Data moves between devices by JAX's collectives and lax.ppermute only.
A program may use at most 64 MiB of HBM per device.

v0:
```python
import math
import jax
import jax.numpy as jnp
from jax import lax
from jax.sharding import PartitionSpec as P

HEADS = 16


def layer_norm(values):
    center = values - jnp.mean(values, axis=-1, keepdims=True)
    spread = jnp.mean(center * center, axis=-1, keepdims=True)
    return center * lax.rsqrt(spread + 1e-06)


def on_device(tokens, w_qkv, w_attn_out, slot_keys, w_expert_in, w_expert_out):
    image_count, length, model_width = tokens.shape
    head_count = HEADS
    head_width = model_width // head_count
    row_count = image_count * length
    normed = (
        layer_norm(tokens.astype(jnp.float32)).astype(jnp.bfloat16).reshape(row_count, model_width)
    )
    full_qkv = lax.all_gather(w_qkv, "expert", axis=0, tiled=True)
    qkv = jnp.dot(normed, full_qkv, preferred_element_type=jnp.float32)
    packed = qkv.astype(jnp.bfloat16).reshape(image_count, length, 3, head_count, head_width)
    query = packed[:, :, 0]
    keys = packed[:, :, 1]
    values = packed[:, :, 2]
    scores = jnp.einsum(
        "bqhd,bkhd->bhqk", query, keys, preferred_element_type=jnp.float32
    ) / math.sqrt(head_width)
    weights = jax.nn.softmax(scores, axis=-1).astype(jnp.bfloat16)
    attended = jnp.einsum(
        "bhqk,bkhd->bqhd", weights, values, preferred_element_type=jnp.float32
    ).astype(jnp.bfloat16)
    attended = attended.reshape(row_count, model_width)
    full_out = lax.all_gather(w_attn_out, "expert", axis=0, tiled=True)
    projected = jnp.dot(attended, full_out, preferred_element_type=jnp.float32)
    resid = tokens.astype(jnp.float32) + projected.reshape(image_count, length, model_width)
    normed_two = layer_norm(resid).astype(jnp.bfloat16)
    slot_count = slot_keys.shape[1]
    logits = jnp.dot(
        normed_two.reshape(row_count, model_width), slot_keys, preferred_element_type=jnp.float32
    )
    logits = logits.reshape(image_count, length, slot_count)
    dispatch = jax.nn.softmax(logits, axis=1).astype(jnp.bfloat16)
    combine = jax.nn.softmax(logits, axis=2).astype(jnp.bfloat16)
    slot_inputs = jnp.einsum(
        "bsn,bsd->bnd", dispatch, normed_two, preferred_element_type=jnp.float32
    ).astype(jnp.bfloat16)
    sources = lax.axis_size("expert")
    expert_here = w_expert_in.shape[0]
    pairs = slot_count // (sources * expert_here)
    block = lax.all_to_all(slot_inputs, "expert", split_axis=1, concat_axis=1, tiled=True)
    batch = block.shape[0]
    arranged = block.reshape(batch, sources, expert_here, pairs, model_width)
    hidden = jnp.einsum(
        "bnepd,edh->bneph", arranged, w_expert_in, preferred_element_type=jnp.float32
    )
    hidden = jax.nn.gelu(hidden, approximate=False).astype(jnp.bfloat16)
    answer = jnp.einsum(
        "bneph,ehd->bnepd", hidden, w_expert_out, preferred_element_type=jnp.float32
    )
    answered = answer.astype(jnp.bfloat16).reshape(batch, slot_count, model_width)
    slot_outputs = lax.all_to_all(answered, "expert", split_axis=1, concat_axis=1, tiled=True)
    mixed = jnp.einsum("bsn,bnd->bsd", combine, slot_outputs, preferred_element_type=jnp.float32)
    return (resid + mixed).astype(jnp.bfloat16)


def solution(mesh):
    placed = (
        P(("group", "expert"), None, None),
        P("expert", None),
        P("expert", None),
        P(),
        P("expert", None, None),
        P("expert", None, None),
    )
    return jax.shard_map(
        on_device,
        mesh=mesh,
        in_specs=placed,
        out_specs=P(("group", "expert"), None, None),
        check_vma=False,
    )
```

profile of v0, /device:TPU:0, one launch (start us, length us, event | category | flops | bytes accessed | tf_op | source)
XLA Modules:
  0.0 159.9 jit_solution(4813306679087702941)
XLA Ops:
  6.5 0.0 copy-start
  6.5 0.0 copy-start.1
  6.5 0.0 all-gather.3.cloned.1.call-start
  6.5 0.7 all-gather.3.cloned.1.call-update
  7.3 0.0 all-gather.5.cloned.1.call-start
  7.3 0.7 all-gather.5.cloned.1.call-update
  8.0 1.4 convert_reduce_fusion
  9.5 0.0 copy-done.1
  9.5 0.4 fusion.14
  9.9 0.3 fusion.15
  10.2 64.0 %all-gather.3.cloned.1.call-done = bf16[1024,3072]{1,0:T(8,128)(2,1)} async-done(((bf16[64,3072]{1,0:T(8,128)(2,1)}), bf16[1024,3072]{1,0:T(8,128)(2,1)}) %all-gather.3.cloned.1.call-update) | async-done | bytes 6291472 | tf_op jit(solution)/shard_map/all_gather | solution.py:24
  74.2 7.5 %convolution_convert_fusion = bf16[512,3072]{1,0:T(8,128)(2,1)} fusion(bf16[512,1024]{1,0:T(8,128)(2,1)S(1)} %bitcast.133, bf16[1024,3072]{1,0:T(8,128)(2,1)} %all-gather.3.cloned.1.call-done), kind=kOutput, calls=%fused_computation.7 | convolution fusion | flops 3222798336 | bytes 10485760 | tf_op jit(solution)/shard_map/dot_general | solution.py:25
  81.8 8.6 %reshape.80 = bf16[2,256,3,16,64]{4,3,2,1,0:T(8,128)(2,1)} reshape(bf16[512,3072]{1,0:T(8,128)(2,1)} %convolution_convert_fusion) | data formatting | bytes 6291456 | tf_op jit(solution)/shard_map/reshape | solution.py:26
  90.4 6.0 %fusion.110 = (bf16[2,256,1,16,64]{4,3,2,1,0:T(8,128)(2,1)S(1)}, bf16[2,256,1,16,64]{4,3,2,1,0:T(8,128)(2,1)}, bf16[2,256,1,16,64]{4,3,2,1,0:T(8,128)(2,1)}) fusion(bf16[2,256,3,16,64]{4,3,2,1,0:T(8,128)(2,1)} %reshape.80), kind=kLoop, calls=%fused_computation.118 | loop fusion | bytes 6291456 | tf_op jit(solution)/shard_map/slice | solution.py:29
  96.4 3.6 %copy.48 = bf16[2,256,1,16,64]{1,4,3,0,2:T(8,128)(2,1)} copy(bf16[2,256,1,16,64]{4,3,2,1,0:T(8,128)(2,1)} %get-tuple-element.6) | data formatting | bytes 2097152
  99.9 3.5 %copy.49 = bf16[2,256,1,16,64]{1,4,3,0,2:T(8,128)(2,1)} copy(bf16[2,256,1,16,64]{4,3,2,1,0:T(8,128)(2,1)} %get-tuple-element.7) | data formatting | bytes 2097152
  103.5 2.5 %copy.47 = bf16[2,256,1,16,64]{1,4,3,0,2:T(8,128)(2,1)} copy(bf16[2,256,1,16,64]{4,3,2,1,0:T(8,128)(2,1)S(1)} %get-tuple-element.5) | data formatting | bytes 2097152
  106.0 2.8 %fusion.31 = f32[2,16,256,256]{2,3,1,0:T(8,128)S(1)} fusion(bf16[2,256,1,16,64]{1,4,3,0,2:T(8,128)(2,1)} %copy.49, bf16[2,256,1,16,64]{1,4,3,0,2:T(8,128)(2,1)} %copy.48), kind=kOutput, calls=%fused_computation.34 | convolution fusion | flops 268435456 | bytes 10485760 | tf_op jit(solution)/shard_map/bqhd,bkhd->bhqk/dot_general | solution.py:30
  108.8 0.0 copy-start.2
  108.8 6.3 %fusion.111 = (f32[2,16,256]{2,1,0:T(8,128)S(1)}, f32[2,16,256,256]{2,3,1,0:T(8,128)S(1)}) fusion(f32[2,16,256,256]{2,3,1,0:T(8,128)S(1)} %fusion.31), kind=kOutput, calls=%fused_computation.119 | output fusion | flops 8388863 | bytes 16809984 | tf_op jit(solution)/shard_map/sub | solution.py:33
  115.1 0.0 copy-done.2
  115.1 1.8 %fusion.20 = bf16[2,16,64,256]{3,2,1,0:T(8,128)(2,1)} fusion(f32[2,16,256,256]{2,3,1,0:T(8,128)S(1)} %get-tuple-element.9, f32[2,16,256]{2,1,0:T(8,128)S(1)} %get-tuple-element.8, bf16[2,256,1,16,64]{1,4,3,0,2:T(8,128)(2,1)S(1)} %copy-done.2), kind=kOutput, calls=%fused_computation.26 | convolution fusion | flops 273154048 | bytes 10518528 | tf_op jit(solution)/shard_map/bhqk,bkhd->bqhd/dot_general | solution.py:34
  117.0 0.0 all-gather.5.cloned.1.call-done
  117.0 3.3 %fusion.112 = (f32[2,256]{1,0:T(2,128)S(1)}, f32[2,256,1024]{2,1,0:T(8,128)S(1)}) fusion(bf16[2,256,1024]{1,2,0:T(8,128)(2,1)} %bitcast.134, bf16[1024,1024]{1,0:T(8,128)(2,1)} %all-gather.5.cloned.1.call-done, bf16[2,256,1024]{2,1,0:T(8,128)(2,1)S(1)} %copy-done.1), kind=kOutput, calls=%fused_computation.120 | convolution fusion | flops 1075314176 | bytes 6293504 | tf_op jit(solution)/shard_map/dot_general | solution.py:39
  120.2 0.4 multiply_reduce_fusion.1
  120.6 0.0 copy-done
  120.6 0.5 fusion.54
  121.2 0.2 fusion.113
  121.3 0.5 convolution_convert_fusion.1
  121.8 0.1 copy.37
  122.0 11.3 %all_to_all.10 = bf16[2,32,1024]{2,0,1:T(2,128)(2,1)S(1)} all-to-all(bf16[2,32,1024]{2,0,1:T(2,128)(2,1)S(1)} %copy.37), channel_id=1, replica_groups=mesh['group'=2,'expert'=16] {'expert'}, dimensions={1} | all-to-all | bytes 262144 | tf_op jit(solution)/shard_map/all_to_all | solution.py:55
  133.2 6.1 %fusion.24 = bf16[2,16,1,2,1024]{4,1,3,0,2:T(8,128)(2,1)S(1)} fusion(bf16[1,2048,1024]{2,1,0:T(8,128)(2,1)} %param.11, bf16[1,1024,2048]{2,1,0:T(8,128)(2,1)} %param.10, bf16[2,16,2,1024]{3,0,2,1:T(2,128)(2,1)S(1)} %bitcast.135), kind=kOutput, calls=%fused_computation.29 | convolution fusion | flops 545456128 | bytes 8650752 | tf_op jit(solution)/shard_map/bneph,ehd->bnepd/dot_general | solution.py:62
  139.3 0.8 copy.39
  140.1 3.5 %all-to-all-start.1 = ((bf16[2,32,1024]{2,0,1:T(2,128)(2,1)}), bf16[2,32,1024]{2,0,1:T(2,128)(2,1)S(1)}, u32[]{:S(2)}, u32[]{:S(2)}) async-start(bf16[2,32,1024]{2,0,1:T(2,128)(2,1)} %bitcast.27), calls=%async_computation.1 | async-start | bytes 262144 | tf_op jit(solution)/shard_map/all_to_all | solution.py:66
  143.7 7.9 %all-to-all-done.1 = bf16[2,32,1024]{2,0,1:T(2,128)(2,1)S(1)} async-done(((bf16[2,32,1024]{2,0,1:T(2,128)(2,1)}), bf16[2,32,1024]{2,0,1:T(2,128)(2,1)S(1)}, u32[]{:S(2)}, u32[]{:S(2)}) %all-to-all-start.1) | async-done | bytes 131104 | tf_op jit(solution)/shard_map/all_to_all | solution.py:66
  151.6 1.5 add_convert_fusion
  (5 shorter events, 0.1 us)
Async XLA Ops:
  6.5 114.1 %copy-start = (bf16[1024,32]{0,1:T(8,128)(2,1)S(1)}, bf16[1024,32]{0,1:T(8,128)(2,1)}, u32[]{:S(2)}) copy-start(bf16[1024,32]{0,1:T(8,128)(2,1)} %param.9) | copy-start | bytes 196612
  6.5 2.9 %copy-start.1 = (bf16[2,256,1024]{2,1,0:T(8,128)(2,1)S(1)}, bf16[2,256,1024]{2,1,0:T(8,128)(2,1)}, u32[]{:S(2)}) copy-start(bf16[2,256,1024]{2,1,0:T(8,128)(2,1)} %param.6) | copy-start | bytes 3145732
  6.5 67.7 %all-gather.3.cloned.1.call-start = ((), (), s32[]{:S(2)}) async-start(), calls=%async_computation.2 | async-start | bytes 6684672 | tf_op jit(solution)/shard_map/all_gather | solution.py:24
  7.3 109.7 %all-gather.5.cloned.1.call-start = ((), (), s32[]{:S(2)}) async-start(), calls=%async_computation.3 | async-start | bytes 2228224 | tf_op jit(solution)/shard_map/all_gather | solution.py:38
  108.8 6.3 %copy-start.2 = (bf16[2,256,1,16,64]{1,4,3,0,2:T(8,128)(2,1)S(1)}, bf16[2,256,1,16,64]{1,4,3,0,2:T(8,128)(2,1)}, u32[]{:S(2)}) copy-start(bf16[2,256,1,16,64]{1,4,3,0,2:T(8,128)(2,1)} %copy.47) | copy-start | bytes 3145732
  140.1 11.4 %all-to-all-start.1 = ((bf16[2,32,1024]{2,0,1:T(2,128)(2,1)}), bf16[2,32,1024]{2,0,1:T(2,128)(2,1)S(1)}, u32[]{:S(2)}, u32[]{:S(2)}) async-start(bf16[2,32,1024]{2,0,1:T(2,128)(2,1)} %bitcast.27), calls=%async_computation.1 | async-start | bytes 262144 | tf_op jit(solution)/shard_map/all_to_all | solution.py:66
Sparse Core Ops, SparseCore 0:
  9.6 64.5 all-gather.2
  76.4 39.9 all-gather.4
where the time goes:
time: 160 us
  waiting for transfers between devices  73.3 us (46%)
  local copies, waits for them, and re-layouts  25.1 us (16%)
  matrix products  24 us (15%)
  between operations  13.5 us (8%)
  blocking collectives  11.3 us (7%)
  other arithmetic  9.08 us (6%)
  starting transfers between devices  3.55 us (2%)
    all_gather x1, waiting for transfers between devices, on_device(): full_qkv = lax.all_gather(w_qkv, 'expert', axis=0, tiled=True)  64 us
    all_to_all x1, blocking collectives, on_device(): lax.all_to_all(slot_inputs, 'expert', split_axis=1, concat_axis=1, tiled=...  11.3 us
    unnamed x9, local copies, waits for them, and re-layouts  9.61 us
    reshape x1, local copies, waits for them, and re-layouts, on_device(): qkv.astype(jnp.bfloat16)  8.6 us
    all_to_all x1, waiting for transfers between devices, on_device(): lax.all_to_all(answered, 'expert', split_axis=1, concat_axis=1, tiled=True)  7.85 us
    dot_general x1, matrix products, on_device(): qkv = jnp.dot(normed, full_qkv, preferred_element_type=jnp.float32)  7.53 us
    sub x1, other arithmetic, on_device(): weights = jax.nn.softmax(scores, axis=-1).astype(jnp.bfloat16)  6.31 us
    dot_general x1, matrix products, on_device(): jnp.einsum('bneph,ehd->bnepd', hidden, w_expert_out, preferred_element_ty...  6.09 us
  transfers between devices with their start and end apart: 3, of which 2 were waited for; matrix products, arithmetic and copies ran while one was open for 28% of the time, Pallas kernels for 0%

commit v1 on v0

--- a/solution.py
+++ b/solution.py
@@ -5,6 +5,28 @@
 from jax.sharding import PartitionSpec as P
 
 HEADS = 16
+
+
+def laid_out(pieces, dim):
+    pieces = jnp.moveaxis(pieces, 0, dim)
+    shape = pieces.shape
+    return pieces.reshape(*shape[:dim], shape[dim] * shape[dim + 1], *shape[dim + 2 :])
+
+
+def collect(shard, axis, dim):
+    size = lax.axis_size(axis)
+    pairs = [(i, (i + 1) % size) for i in range(size)]
+    back = [(b, a) for a, b in pairs]
+    lower, upper = ([], [])
+    for step in range(size - 1):
+        if step % 2 == 0:
+            lower.append(lax.ppermute(lower[-1] if lower else shard, axis, pairs))
+        else:
+            upper.append(lax.ppermute(upper[-1] if upper else shard, axis, back))
+    blocks = jnp.stack([*lower[::-1], shard, *upper])
+    shift = lax.axis_index(axis) - len(lower)
+    blocks = blocks[(jnp.arange(size) - shift) % size]
+    return laid_out(blocks, dim)
 
 
 def layer_norm(values):
@@ -21,7 +43,7 @@
     normed = (
         layer_norm(tokens.astype(jnp.float32)).astype(jnp.bfloat16).reshape(row_count, model_width)
     )
-    full_qkv = lax.all_gather(w_qkv, "expert", axis=0, tiled=True)
+    full_qkv = collect(w_qkv, "expert", 0)
     qkv = jnp.dot(normed, full_qkv, preferred_element_type=jnp.float32)
     packed = qkv.astype(jnp.bfloat16).reshape(image_count, length, 3, head_count, head_width)
     query = packed[:, :, 0]

time: 160 us -> 201 us (1.26)
  starting transfers between devices: 3.55 us -> 36.2 us
  waiting for transfers between devices: 73.3 us -> 53 us
  local copies, waits for them, and re-layouts: 25.1 us -> 43.2 us
  blocking collectives: 11.3 us -> 18.8 us
  other arithmetic: 9.08 us -> 12.6 us
    all_gather x1 -> x0, waiting for transfers between devices: 64 us -> none  [on_device(): full_qkv = lax.all_gather(w_qkv, 'expert', axis=0, tiled=True)]
    ppermute x0 -> x15, waiting for transfers between devices: none -> 45.1 us  [the longest x8 45.1 us: collect(): lower.append(lax.ppermute(lower[-1] if lower else shard, axis, pairs))]
    ppermute x0 -> x15, starting transfers between devices: none -> 32.7 us  [the longest x7 28.1 us: collect(): upper.append(lax.ppermute(upper[-1] if upper else shard, axis, back))]
    unnamed x9 -> x30, local copies, waits for them, and re-layouts: 9.61 us -> 22.9 us
    all_to_all x1, blocking collectives: 11.3 us -> 18.8 us  [on_device(): lax.all_to_all(slot_inputs, 'expert', split_axis=1, concat_axis=1, tiled=...]
    gather x0 -> x1, local copies, waits for them, and re-layouts: none -> 6.39 us  [collect(): blocks = blocks[(jnp.arange(size) - shift) % size]]
    reshape x1, local copies, waits for them, and re-layouts: 8.6 us -> 6.12 us  [on_device(): qkv.astype(jnp.bfloat16)]
    convert_element_type x1, other arithmetic: 0.32 us -> 2.5 us  [on_device(): layer_norm(tokens.astype(jnp.float32)).astype(jnp.bfloat16)]
  transfers between devices with their start and end apart: 3 -> 17, of which waited for: 2 -> 9; matrix products, arithmetic and copies ran while one was open for 28% -> 32% of each run, Pallas kernels for 0% -> 0%
where the time goes in v1:
time: 201 us; the launch traced here: 200 us
  waiting for transfers between devices  53 us (26%)
  local copies, waits for them, and re-layouts  43.2 us (21%)
  starting transfers between devices  36.2 us (18%)
  matrix products  22.7 us (11%)
  blocking collectives  18.8 us (9%)
  between operations  13.5 us (7%)
  other arithmetic  12.6 us (6%)
    ppermute x8, waiting for transfers between devices, collect(): lower.append(lax.ppermute(lower[-1] if lower else shard, axis, pairs))  45.1 us
    ppermute x7, starting transfers between devices, collect(): upper.append(lax.ppermute(upper[-1] if upper else shard, axis, back))  28.1 us
    unnamed x30, local copies, waits for them, and re-layouts  22.9 us
    all_to_all x1, blocking collectives, on_device(): lax.all_to_all(slot_inputs, 'expert', split_axis=1, concat_axis=1, tiled=...  18.8 us
    all_to_all x1, waiting for transfers between devices, on_device(): lax.all_to_all(answered, 'expert', split_axis=1, concat_axis=1, tiled=True)  7.85 us
    dot_general x1, matrix products, on_device(): qkv = jnp.dot(normed, full_qkv, preferred_element_type=jnp.float32)  6.54 us
    gather x1, local copies, waits for them, and re-layouts, collect(): blocks = blocks[(jnp.arange(size) - shift) % size]  6.39 us
    sub x1, other arithmetic, on_device(): weights = jax.nn.softmax(scores, axis=-1).astype(jnp.bfloat16)  6.31 us
  transfers between devices with their start and end apart: 17, of which 9 were waited for; matrix products, arithmetic and copies ran while one was open for 32% of the time, Pallas kernels for 0%

profile of v1, /device:TPU:0, one launch (start us, length us, event | category | flops | bytes accessed | tf_op | source)
XLA Modules:
  0.0 200.1 jit_solution(4644941336463404335)
XLA Ops:
  6.5 0.5 collective-permute-start
  7.0 10.7 %collective-permute-done = bf16[64,3072]{1,0:T(8,128)(2,1)S(1)} collective-permute-done((bf16[64,3072]{1,0:T(8,128)(2,1)}, bf16[64,3072]{1,0:T(8,128)(2,1)S(1)}, u32[]{:S(2)}, u32[]{:S(2)}) %collective-permute-start) | collective-permute-done | bytes 393248 | tf_op jit(solution)/shard_map/ppermute | solution.py:23
  17.7 4.4 %collective-permute-start.8 = (bf16[64,3072]{1,0:T(8,128)(2,1)}, bf16[64,3072]{1,0:T(8,128)(2,1)S(1)}, u32[]{:S(2)}, u32[]{:S(2)}) collective-permute-start(bf16[64,3072]{1,0:T(8,128)(2,1)} %param.7), channel_id=1, source_target_pairs={{1,0},{2,1},{3,2},{4,3},{5,4},{6,5},{7,6},{8,7},{9,8},{10,9},{11,1... | collective-permute-start | bytes 1179656 | tf_op jit(solution)/shard_map/ppermute | solution.py:25
  22.1 5.6 %collective-permute-done.1 = bf16[64,3072]{1,0:T(8,128)(2,1)S(1)} collective-permute-done((bf16[64,3072]{1,0:T(8,128)(2,1)S(1)}, bf16[64,3072]{1,0:T(8,128)(2,1)S(1)}, u32[]{:S(2)}, u32[]{:S(2)}) %collective-permute-start.1) | collective-permute-done | bytes 393248 | tf_op jit(solution)/shard_map/ppermute | solution.py:23
  27.7 0.0 collective-permute-done.8
  27.7 4.6 %collective-permute-start.9 = (bf16[64,3072]{1,0:T(8,128)(2,1)S(1)}, bf16[64,3072]{1,0:T(8,128)(2,1)S(1)}, u32[]{:S(2)}, u32[]{:S(2)}) collective-permute-start(bf16[64,3072]{1,0:T(8,128)(2,1)S(1)} %collective-permute-done.8), channel_id=1, source_target_pairs={{1,0},{2,1},{3,2},{4,3},{5,4},{6,5},{7,6},{8,7},{9,8},{10,9},{11,1... | collective-permute-start | bytes 1179656 | tf_op jit(solution)/shard_map/ppermute | solution.py:25
  32.3 5.4 %collective-permute-done.2 = bf16[64,3072]{1,0:T(8,128)(2,1)S(1)} collective-permute-done((bf16[64,3072]{1,0:T(8,128)(2,1)S(1)}, bf16[64,3072]{1,0:T(8,128)(2,1)S(1)}, u32[]{:S(2)}, u32[]{:S(2)}) %collective-permute-start.2) | collective-permute-done | bytes 393248 | tf_op jit(solution)/shard_map/ppermute | solution.py:23
  37.7 4.6 %collective-permute-start.10 = (bf16[64,3072]{1,0:T(8,128)(2,1)S(1)}, bf16[64,3072]{1,0:T(8,128)(2,1)S(1)}, u32[]{:S(2)}, u32[]{:S(2)}) collective-permute-start(bf16[64,3072]{1,0:T(8,128)(2,1)S(1)} %collective-permute-done.9), channel_id=1, source_target_pairs={{1,0},{2,1},{3,2},{4,3},{5,4},{6,5},{7,6},{8,7},{9,8},{10,9},{11,1... | collective-permute-start | bytes 1179656 | tf_op jit(solution)/shard_map/ppermute | solution.py:25
  42.3 5.4 %collective-permute-done.3 = bf16[64,3072]{1,0:T(8,128)(2,1)S(1)} collective-permute-done((bf16[64,3072]{1,0:T(8,128)(2,1)S(1)}, bf16[64,3072]{1,0:T(8,128)(2,1)S(1)}, u32[]{:S(2)}, u32[]{:S(2)}) %collective-permute-start.3) | collective-permute-done | bytes 393248 | tf_op jit(solution)/shard_map/ppermute | solution.py:23
  47.7 0.3 collective-permute-start.4
  48.0 0.4 copy-done.4
  48.5 3.9 %collective-permute-start.11 = (bf16[64,3072]{1,0:T(8,128)(2,1)S(1)}, bf16[64,3072]{1,0:T(8,128)(2,1)S(1)}, u32[]{:S(2)}, u32[]{:S(2)}) collective-permute-start(bf16[64,3072]{1,0:T(8,128)(2,1)S(1)} %collective-permute-done.10), channel_id=1, source_target_pairs={{1,0},{2,1},{3,2},{4,3},{5,4},{6,5},{7,6},{8,7},{9,8},{10,9},{11,1... | collective-permute-start | bytes 1179656 | tf_op jit(solution)/shard_map/ppermute | solution.py:25
  52.4 5.5 %collective-permute-done.4 = bf16[64,3072]{1,0:T(8,128)(2,1)} collective-permute-done((bf16[64,3072]{1,0:T(8,128)(2,1)S(1)}, bf16[64,3072]{1,0:T(8,128)(2,1)}, u32[]{:S(2)}, u32[]{:S(2)}) %collective-permute-start.4) | collective-permute-done | bytes 393248 | tf_op jit(solution)/shard_map/ppermute | solution.py:23
  57.8 0.9 collective-permute-start.5
  58.7 0.0 all-gather.2.cloned.1.call-update
  58.7 1.5 convert_reduce_fusion
  60.2 3.6 %collective-permute-start.12 = (bf16[64,3072]{1,0:T(8,128)(2,1)S(1)}, bf16[64,3072]{1,0:T(8,128)(2,1)S(1)}, u32[]{:S(2)}, u32[]{:S(2)}) collective-permute-start(bf16[64,3072]{1,0:T(8,128)(2,1)S(1)} %collective-permute-done.11), channel_id=1, source_target_pairs={{1,0},{2,1},{3,2},{4,3},{5,4},{6,5},{7,6},{8,7},{9,8},{10,9},{11,1... | collective-permute-start | bytes 1179656 | tf_op jit(solution)/shard_map/ppermute | solution.py:25
  63.9 4.3 %collective-permute-done.5 = bf16[64,3072]{1,0:T(8,128)(2,1)} collective-permute-done((bf16[64,3072]{1,0:T(8,128)(2,1)}, bf16[64,3072]{1,0:T(8,128)(2,1)}, u32[]{:S(2)}, u32[]{:S(2)}) %collective-permute-start.5) | collective-permute-done | bytes 393248 | tf_op jit(solution)/shard_map/ppermute | solution.py:23
  68.1 2.5 %collective-permute-start.6 = (bf16[64,3072]{1,0:T(8,128)(2,1)}, bf16[64,3072]{1,0:T(8,128)(2,1)S(1)}, u32[]{:S(2)}, u32[]{:S(2)}) collective-permute-start(bf16[64,3072]{1,0:T(8,128)(2,1)} %collective-permute-done.5), channel_id=1, source_target_pairs={{0,1},{1,2},{2,3},{3,4},{4,5},{5,6},{6,7},{7,8},{8,9},{9,10},{10,1... | collective-permute-start | bytes 1179656 | tf_op jit(solution)/shard_map/ppermute | solution.py:23
  70.6 1.6 fusion.14
  72.3 3.0 %collective-permute-start.13 = (bf16[64,3072]{1,0:T(8,128)(2,1)S(1)}, bf16[64,3072]{1,0:T(8,128)(2,1)S(1)}, u32[]{:S(2)}, u32[]{:S(2)}) collective-permute-start(bf16[64,3072]{1,0:T(8,128)(2,1)S(1)} %collective-permute-done.12), channel_id=1, source_target_pairs={{1,0},{2,1},{3,2},{4,3},{5,4},{6,5},{7,6},{8,7},{9,8},{10,9},{11,1... | collective-permute-start | bytes 1179656 | tf_op jit(solution)/shard_map/ppermute | solution.py:25
  75.2 5.3 %collective-permute-done.6 = bf16[64,3072]{1,0:T(8,128)(2,1)S(1)} collective-permute-done((bf16[64,3072]{1,0:T(8,128)(2,1)}, bf16[64,3072]{1,0:T(8,128)(2,1)S(1)}, u32[]{:S(2)}, u32[]{:S(2)}) %collective-permute-start.6) | collective-permute-done | bytes 393248 | tf_op jit(solution)/shard_map/ppermute | solution.py:23
  80.5 0.4 collective-permute-start.7
  81.0 2.5 %fusion.15 = bf16[2,256,1024]{2,1,0:T(8,128)(2,1)} fusion(bf16[2,256,1024]{2,1,0:T(8,128)(2,1)} %param.6, f32[2,256]{1,0:T(2,128)S(1)} %add_rsqrt_fusion.1, f32[2,256]{1,0:T(2,128)S(1)} %broadcast_multiply_fusion.1), kind=kLoop, calls=%fused_computation.21 | loop fusion | flops 2097152 | bytes 2101248 | tf_op jit(solution)/shard_map/convert_element_type | solution.py:44
  83.5 4.0 %collective-permute-start.14 = (bf16[64,3072]{1,0:T(8,128)(2,1)S(1)}, bf16[64,3072]{1,0:T(8,128)(2,1)S(1)}, u32[]{:S(2)}, u32[]{:S(2)}) collective-permute-start(bf16[64,3072]{1,0:T(8,128)(2,1)S(1)} %collective-permute-done.13), channel_id=1, source_target_pairs={{1,0},{2,1},{3,2},{4,3},{5,4},{6,5},{7,6},{8,7},{9,8},{10,9},{11,1... | collective-permute-start | bytes 1179656 | tf_op jit(solution)/shard_map/ppermute | solution.py:25
  87.5 3.0 %collective-permute-done.7 = bf16[64,3072]{1,0:T(8,128)(2,1)S(1)} collective-permute-done((bf16[64,3072]{1,0:T(8,128)(2,1)S(1)}, bf16[64,3072]{1,0:T(8,128)(2,1)S(1)}, u32[]{:S(2)}, u32[]{:S(2)}) %collective-permute-start.7) | collective-permute-done | bytes 393248 | tf_op jit(solution)/shard_map/ppermute | solution.py:23
  90.6 0.8 bitcast_dynamic-update-slice_fusion.15
  91.3 0.8 bitcast_dynamic-update-slice_fusion.14
  92.1 1.8 bitcast_dynamic-update-slice_fusion.13
  93.9 1.8 bitcast_dynamic-update-slice_fusion.12
  95.7 0.8 bitcast_dynamic-update-slice_fusion.11
  96.4 0.8 bitcast_dynamic-update-slice_fusion.10
  97.2 0.8 bitcast_dynamic-update-slice_fusion.9
  98.0 0.8 bitcast_dynamic-update-slice_fusion.8
  98.8 0.8 bitcast_dynamic-update-slice_fusion.7
  99.6 0.8 bitcast_dynamic-update-slice_fusion.6
  100.3 0.8 bitcast_dynamic-update-slice_fusion.5
  101.1 0.8 bitcast_dynamic-update-slice_fusion.4
  101.9 0.8 bitcast_dynamic-update-slice_fusion.3
  102.6 0.8 bitcast_dynamic-update-slice_fusion.2
  103.4 0.8 bitcast_dynamic-update-slice_fusion.1
  104.2 0.8 bitcast_dynamic-update-slice_fusion
  105.0 6.4 %gather_fusion = bf16[16,64,3072]{2,1,0:T(8,128)(2,1)} fusion(bf16[16,64,3072]{2,1,0:T(8,128)(2,1)} %bitcast_dynamic-update-slice_fusion, s32[1024]{0:T(1024)S(1)} %pad_clamp_fusion), kind=kCustom, calls=%fused_computation | custom fusion | bytes 12582976 | tf_op jit(solution)/shard_map/gather | solution.py:28
  111.4 6.5 %convolution_convert_fusion = bf16[512,3072]{1,0:T(8,128)(2,1)S(1)} fusion(bf16[512,1024]{1,0:T(8,128)(2,1)} %bitcast.169, bf16[1024,3072]{1,0:T(8,128)(2,1)} %bitcast.168), kind=kOutput, calls=%fused_computation.8 | convolution fusion | flops 3222798336 | bytes 10485760 | tf_op jit(solution)/shard_map/dot_general | solution.py:47
  117.9 6.1 %reshape.141 = bf16[2,256,3,16,64]{4,3,2,1,0:T(8,128)(2,1)} reshape(bf16[512,3072]{1,0:T(8,128)(2,1)S(1)} %convolution_convert_fusion) | data formatting | bytes 6291456 | tf_op jit(solution)/shard_map/reshape | solution.py:48
  124.1 6.0 %fusion.112 = (bf16[2,256,1,16,64]{4,3,2,1,0:T(8,128)(2,1)S(1)}, bf16[2,256,1,16,64]{4,3,2,1,0:T(8,128)(2,1)}, bf16[2,256,1,16,64]{4,3,2,1,0:T(8,128)(2,1)}) fusion(bf16[2,256,3,16,64]{4,3,2,1,0:T(8,128)(2,1)} %reshape.141), kind=kLoop, calls=%fused_computation.142 | loop fusion | bytes 6291456 | tf_op jit(solution)/shard_map/slice | solution.py:51
  130.1 2.8 %copy.48 = bf16[2,256,1,16,64]{1,4,3,0,2:T(8,128)(2,1)S(1)} copy(bf16[2,256,1,16,64]{4,3,2,1,0:T(8,128)(2,1)} %get-tuple-element.6) | data formatting | bytes 2097152
  132.9 3.6 %copy.49 = bf16[2,256,1,16,64]{1,4,3,0,2:T(8,128)(2,1)} copy(bf16[2,256,1,16,64]{4,3,2,1,0:T(8,128)(2,1)} %get-tuple-element.7) | data formatting | bytes 2097152
  136.4 2.5 %copy.47 = bf16[2,256,1,16,64]{1,4,3,0,2:T(8,128)(2,1)} copy(bf16[2,256,1,16,64]{4,3,2,1,0:T(8,128)(2,1)S(1)} %get-tuple-element.5) | data formatting | bytes 2097152
  138.9 2.5 %fusion.31 = f32[2,16,256,256]{2,3,1,0:T(8,128)S(1)} fusion(bf16[2,256,1,16,64]{1,4,3,0,2:T(8,128)(2,1)} %copy.49, bf16[2,256,1,16,64]{1,4,3,0,2:T(8,128)(2,1)S(1)} %copy.48), kind=kOutput, calls=%fused_computation.35 | convolution fusion | flops 268435456 | bytes 10485760 | tf_op jit(solution)/shard_map/bqhd,bkhd->bhqk/dot_general | solution.py:52
  141.5 6.3 %fusion.113 = (f32[2,16,256]{2,1,0:T(8,128)S(1)}, f32[2,16,256,256]{2,3,1,0:T(8,128)S(1)}) fusion(f32[2,16,256,256]{2,3,1,0:T(8,128)S(1)} %fusion.31), kind=kOutput, calls=%fused_computation.143 | output fusion | flops 8388863 | bytes 16809984 | tf_op jit(solution)/shard_map/sub | solution.py:55
  147.8 1.8 fusion.20
  149.6 3.3 %fusion.114 = (f32[2,256]{1,0:T(2,128)S(1)}, f32[2,256,1024]{2,1,0:T(8,128)S(1)}) fusion(bf16[2,256,1024]{1,2,0:T(8,128)(2,1)} %bitcast.170, bf16[1024,1024]{1,0:T(8,128)(2,1)} %all-gather.2.cloned.1.call-done, bf16[2,256,1024]{2,1,0:T(8,128)(2,1)S(1)} %copy-done.1), kind=kOutput, calls=%fused_computation.144 | convolution fusion | flops 1075314176 | bytes 6293504 | tf_op jit(solution)/shard_map/dot_general | solution.py:61
  152.9 0.4 multiply_reduce_fusion.1
  153.3 0.5 fusion.54
  153.8 0.2 fusion.115
  154.0 0.5 convolution_convert_fusion.1
  154.5 0.1 copy.37
  154.6 18.8 %all_to_all.10 = bf16[2,32,1024]{2,0,1:T(2,128)(2,1)S(1)} all-to-all(bf16[2,32,1024]{2,0,1:T(2,128)(2,1)S(1)} %copy.37), channel_id=1, replica_groups=mesh['group'=2,'expert'=16] {'expert'}, dimensions={1} | all-to-all | bytes 262144 | tf_op jit(solution)/shard_map/all_to_all | solution.py:77
  173.5 6.1 %fusion.24 = bf16[2,16,1,2,1024]{4,1,3,0,2:T(8,128)(2,1)S(1)} fusion(bf16[1,2048,1024]{2,1,0:T(8,128)(2,1)} %param.11, bf16[1,1024,2048]{2,1,0:T(8,128)(2,1)} %param.10, bf16[2,16,2,1024]{3,0,2,1:T(2,128)(2,1)S(1)} %bitcast.171), kind=kOutput, calls=%fused_computation.30 | convolution fusion | flops 545456128 | bytes 8650752 | tf_op jit(solution)/shard_map/bneph,ehd->bnepd/dot_general | solution.py:84
  179.6 0.8 copy.39
  180.3 3.5 %all-to-all-start.1 = ((bf16[2,32,1024]{2,0,1:T(2,128)(2,1)}), bf16[2,32,1024]{2,0,1:T(2,128)(2,1)S(1)}, u32[]{:S(2)}, u32[]{:S(2)}) async-start(bf16[2,32,1024]{2,0,1:T(2,128)(2,1)} %bitcast.45), calls=%async_computation.1 | async-start | bytes 262144 | tf_op jit(solution)/shard_map/all_to_all | solution.py:88
  183.9 7.9 %all-to-all-done.1 = bf16[2,32,1024]{2,0,1:T(2,128)(2,1)S(1)} async-done(((bf16[2,32,1024]{2,0,1:T(2,128)(2,1)}), bf16[2,32,1024]{2,0,1:T(2,128)(2,1)S(1)}, u32[]{:S(2)}, u32[]{:S(2)}) %all-to-all-start.1) | async-done | bytes 131104 | tf_op jit(solution)/shard_map/all_to_all | solution.py:88
  191.8 1.5 add_convert_fusion
  (29 shorter events, 0.1 us)
Async XLA Ops:
  6.5 146.7 %copy-start = (bf16[1024,32]{0,1:T(8,128)(2,1)S(1)}, bf16[1024,32]{0,1:T(8,128)(2,1)}, u32[]{:S(2)}) copy-start(bf16[1024,32]{0,1:T(8,128)(2,1)} %param.9) | copy-start | bytes 196612
  6.5 92.2 %copy-start.3 = (bf16[64,3072]{1,0:T(8,128)(2,1)S(1)}, bf16[64,3072]{1,0:T(8,128)(2,1)}, u32[]{:S(2)}) copy-start(bf16[64,3072]{1,0:T(8,128)(2,1)} %param.7) | copy-start | bytes 1179652
  6.5 143.1 %all-gather.2.cloned.1.call-start = ((), (), s32[]{:S(2)}) async-start(), calls=%async_computation.2 | async-start | bytes 2228224 | tf_op jit(solution)/shard_map/all_gather | solution.py:60
  6.5 11.1 %collective-permute-start = (bf16[64,3072]{1,0:T(8,128)(2,1)}, bf16[64,3072]{1,0:T(8,128)(2,1)S(1)}, u32[]{:S(2)}, u32[]{:S(2)}) collective-permute-start(bf16[64,3072]{1,0:T(8,128)(2,1)} %param.7), channel_id=1, source_target_pairs={{0,1},{1,2},{2,3},{3,4},{4,5},{5,6},{6,7},{7,8},{8,9},{9,10},{10,1... | collective-permute-start | bytes 1179656 | tf_op jit(solution)/shard_map/ppermute | solution.py:23
  17.7 10.0 %collective-permute-start.1 = (bf16[64,3072]{1,0:T(8,128)(2,1)S(1)}, bf16[64,3072]{1,0:T(8,128)(2,1)S(1)}, u32[]{:S(2)}, u32[]{:S(2)}) collective-permute-start(bf16[64,3072]{1,0:T(8,128)(2,1)S(1)} %collective-permute-done), channel_id=1, source_target_pairs={{0,1},{1,2},{2,3},{3,4},{4,5},{5,6},{6,7},{7,8},{8,9},{9,10},{10,1... | collective-permute-start | bytes 1179656 | tf_op jit(solution)/shard_map/ppermute | solution.py:23
  17.7 10.1 %collective-permute-start.8 = (bf16[64,3072]{1,0:T(8,128)(2,1)}, bf16[64,3072]{1,0:T(8,128)(2,1)S(1)}, u32[]{:S(2)}, u32[]{:S(2)}) collective-permute-start(bf16[64,3072]{1,0:T(8,128)(2,1)} %param.7), channel_id=1, source_target_pairs={{1,0},{2,1},{3,2},{4,3},{5,4},{6,5},{7,6},{8,7},{9,8},{10,9},{11,1... | collective-permute-start | bytes 1179656 | tf_op jit(solution)/shard_map/ppermute | solution.py:25
  27.7 10.0 %collective-permute-start.2 = (bf16[64,3072]{1,0:T(8,128)(2,1)S(1)}, bf16[64,3072]{1,0:T(8,128)(2,1)S(1)}, u32[]{:S(2)}, u32[]{:S(2)}) collective-permute-start(bf16[64,3072]{1,0:T(8,128)(2,1)S(1)} %collective-permute-done.1), channel_id=1, source_target_pairs={{0,1},{1,2},{2,3},{3,4},{4,5},{5,6},{6,7},{7,8},{8,9},{9,10},{10,1... | collective-permute-start | bytes 1179656 | tf_op jit(solution)/shard_map/ppermute | solution.py:23
  27.7 10.0 %collective-permute-start.9 = (bf16[64,3072]{1,0:T(8,128)(2,1)S(1)}, bf16[64,3072]{1,0:T(8,128)(2,1)S(1)}, u32[]{:S(2)}, u32[]{:S(2)}) collective-permute-start(bf16[64,3072]{1,0:T(8,128)(2,1)S(1)} %collective-permute-done.8), channel_id=1, source_target_pairs={{1,0},{2,1},{3,2},{4,3},{5,4},{6,5},{7,6},{8,7},{9,8},{10,9},{11,1... | collective-permute-start | bytes 1179656 | tf_op jit(solution)/shard_map/ppermute | solution.py:25
  37.7 10.0 %collective-permute-start.3 = (bf16[64,3072]{1,0:T(8,128)(2,1)S(1)}, bf16[64,3072]{1,0:T(8,128)(2,1)S(1)}, u32[]{:S(2)}, u32[]{:S(2)}) collective-permute-start(bf16[64,3072]{1,0:T(8,128)(2,1)S(1)} %collective-permute-done.2), channel_id=1, source_target_pairs={{0,1},{1,2},{2,3},{3,4},{4,5},{5,6},{6,7},{7,8},{8,9},{9,10},{10,1... | collective-permute-start | bytes 1179656 | tf_op jit(solution)/shard_map/ppermute | solution.py:23
  37.7 10.3 %collective-permute-start.10 = (bf16[64,3072]{1,0:T(8,128)(2,1)S(1)}, bf16[64,3072]{1,0:T(8,128)(2,1)S(1)}, u32[]{:S(2)}, u32[]{:S(2)}) collective-permute-start(bf16[64,3072]{1,0:T(8,128)(2,1)S(1)} %collective-permute-done.9), channel_id=1, source_target_pairs={{1,0},{2,1},{3,2},{4,3},{5,4},{6,5},{7,6},{8,7},{9,8},{10,9},{11,1... | collective-permute-start | bytes 1179656 | tf_op jit(solution)/shard_map/ppermute | solution.py:25
  47.7 0.8 copy-start.4
  47.7 10.1 %collective-permute-start.4 = (bf16[64,3072]{1,0:T(8,128)(2,1)S(1)}, bf16[64,3072]{1,0:T(8,128)(2,1)}, u32[]{:S(2)}, u32[]{:S(2)}) collective-permute-start(bf16[64,3072]{1,0:T(8,128)(2,1)S(1)} %collective-permute-done.3), channel_id=1, source_target_pairs={{0,1},{1,2},{2,3},{3,4},{4,5},{5,6},{6,7},{7,8},{8,9},{9,10},{10,1... | collective-permute-start | bytes 1179656 | tf_op jit(solution)/shard_map/ppermute | solution.py:23
  48.5 11.7 %collective-permute-start.11 = (bf16[64,3072]{1,0:T(8,128)(2,1)S(1)}, bf16[64,3072]{1,0:T(8,128)(2,1)S(1)}, u32[]{:S(2)}, u32[]{:S(2)}) collective-permute-start(bf16[64,3072]{1,0:T(8,128)(2,1)S(1)} %collective-permute-done.10), channel_id=1, source_target_pairs={{1,0},{2,1},{3,2},{4,3},{5,4},{6,5},{7,6},{8,7},{9,8},{10,9},{11,1... | collective-permute-start | bytes 1179656 | tf_op jit(solution)/shard_map/ppermute | solution.py:25
  57.8 10.3 %collective-permute-start.5 = (bf16[64,3072]{1,0:T(8,128)(2,1)}, bf16[64,3072]{1,0:T(8,128)(2,1)}, u32[]{:S(2)}, u32[]{:S(2)}) collective-permute-start(bf16[64,3072]{1,0:T(8,128)(2,1)} %collective-permute-done.4), channel_id=1, source_target_pairs={{0,1},{1,2},{2,3},{3,4},{4,5},{5,6},{6,7},{7,8},{8,9},{9,10},{10,1... | collective-permute-start | bytes 1179656 | tf_op jit(solution)/shard_map/ppermute | solution.py:23
  58.7 37.0 %copy-start.5 = (bf16[64,3072]{1,0:T(8,128)(2,1)S(1)}, bf16[64,3072]{1,0:T(8,128)(2,1)}, u32[]{:S(2)}) copy-start(bf16[64,3072]{1,0:T(8,128)(2,1)} %copy-done.4) | copy-start | bytes 1179652
  60.2 12.0 %collective-permute-start.12 = (bf16[64,3072]{1,0:T(8,128)(2,1)S(1)}, bf16[64,3072]{1,0:T(8,128)(2,1)S(1)}, u32[]{:S(2)}, u32[]{:S(2)}) collective-permute-start(bf16[64,3072]{1,0:T(8,128)(2,1)S(1)} %collective-permute-done.11), channel_id=1, source_target_pairs={{1,0},{2,1},{3,2},{4,3},{5,4},{6,5},{7,6},{8,7},{9,8},{10,9},{11,1... | collective-permute-start | bytes 1179656 | tf_op jit(solution)/shard_map/ppermute | solution.py:25
  68.1 12.4 %collective-permute-start.6 = (bf16[64,3072]{1,0:T(8,128)(2,1)}, bf16[64,3072]{1,0:T(8,128)(2,1)S(1)}, u32[]{:S(2)}, u32[]{:S(2)}) collective-permute-start(bf16[64,3072]{1,0:T(8,128)(2,1)} %collective-permute-done.5), channel_id=1, source_target_pairs={{0,1},{1,2},{2,3},{3,4},{4,5},{5,6},{6,7},{7,8},{8,9},{9,10},{10,1... | collective-permute-start | bytes 1179656 | tf_op jit(solution)/shard_map/ppermute | solution.py:23
  72.3 11.3 %collective-permute-start.13 = (bf16[64,3072]{1,0:T(8,128)(2,1)S(1)}, bf16[64,3072]{1,0:T(8,128)(2,1)S(1)}, u32[]{:S(2)}, u32[]{:S(2)}) collective-permute-start(bf16[64,3072]{1,0:T(8,128)(2,1)S(1)} %collective-permute-done.12), channel_id=1, source_target_pairs={{1,0},{2,1},{3,2},{4,3},{5,4},{6,5},{7,6},{8,7},{9,8},{10,9},{11,1... | collective-permute-start | bytes 1179656 | tf_op jit(solution)/shard_map/ppermute | solution.py:25
  80.5 10.0 %collective-permute-start.7 = (bf16[64,3072]{1,0:T(8,128)(2,1)S(1)}, bf16[64,3072]{1,0:T(8,128)(2,1)S(1)}, u32[]{:S(2)}, u32[]{:S(2)}) collective-permute-start(bf16[64,3072]{1,0:T(8,128)(2,1)S(1)} %collective-permute-done.6), channel_id=1, source_target_pairs={{0,1},{1,2},{2,3},{3,4},{4,5},{5,6},{6,7},{7,8},{8,9},{9,10},{10,1... | collective-permute-start | bytes 1179656 | tf_op jit(solution)/shard_map/ppermute | solution.py:23
  83.5 20.7 %collective-permute-start.14 = (bf16[64,3072]{1,0:T(8,128)(2,1)S(1)}, bf16[64,3072]{1,0:T(8,128)(2,1)S(1)}, u32[]{:S(2)}, u32[]{:S(2)}) collective-permute-start(bf16[64,3072]{1,0:T(8,128)(2,1)S(1)} %collective-permute-done.13), channel_id=1, source_target_pairs={{1,0},{2,1},{3,2},{4,3},{5,4},{6,5},{7,6},{8,7},{9,8},{10,9},{11,1... | collective-permute-start | bytes 1179656 | tf_op jit(solution)/shard_map/ppermute | solution.py:25
  141.5 6.3 %copy-start.2 = (bf16[2,256,1,16,64]{1,4,3,0,2:T(8,128)(2,1)S(1)}, bf16[2,256,1,16,64]{1,4,3,0,2:T(8,128)(2,1)}, u32[]{:S(2)}) copy-start(bf16[2,256,1,16,64]{1,4,3,0,2:T(8,128)(2,1)} %copy.47) | copy-start | bytes 3145732
  147.8 1.8 copy-start.1
  180.3 11.4 %all-to-all-start.1 = ((bf16[2,32,1024]{2,0,1:T(2,128)(2,1)}), bf16[2,32,1024]{2,0,1:T(2,128)(2,1)S(1)}, u32[]{:S(2)}, u32[]{:S(2)}) async-start(bf16[2,32,1024]{2,0,1:T(2,128)(2,1)} %bitcast.45), calls=%async_computation.1 | async-start | bytes 262144 | tf_op jit(solution)/shard_map/all_to_all | solution.py:88
Sparse Core Ops, SparseCore 0:
  58.8 46.6 all-gather.1
